TPU v7x, 32 devices: a whole 2x2x4 slice. The times are simulated.
32 devices in a mesh: groups: 2 (over y), row: 8 (over z, x), col: 2 (over core).
Axes of the slice: x: 2, y: 2, z: 4, core: 2. Of those that a mesh axis runs over, the one named last changes fastest.
Arguments:
- object_slices: float32 [4, 2, 2048, 512], P(None, None, ('groups', 'row'), 'col'), parts along dimension 2, may hold values from -4 to 4
- probe: float32 [16, 2, 128, 128], P('groups'), parts along dimension 0, may hold values from -3 to 3
- taps: float32 [2, 63], replicated, may hold values from -0.5 to 0.5
- measured: float32 [64, 128, 128], P(('groups', 'row', 'col')), parts along dimension 0, may hold values from 0.5 to 16
- positions: int32 [64, 2], P(('groups', 'row', 'col')), parts along dimension 0, may hold values from -64 to 959, as said below
Outputs:
- object_grad: float32 [4, 2, 2048, 512], P(None, None, ('groups', 'row'), 'col'), parts along dimension 2
- new_probe: float32 [16, 2, 16384], P('groups', None, ('row', 'col')), parts along dimension 0
There are 2 independent parts, one for each index of `groups`. A program takes and returns all parts, laid end to end along the dimension named above; an argument that names none is the same for every part. Nothing has to cross between parts.
Inputs may be any that keep to these rules, and one draw needn't show every extreme that they name: `positions`: record r belongs to device d = r // 2 in row-major order over the (row, col) device grid, with tile indices (i, q); its row lies in [i * 128 - 128/2, (i + 1) * 128 - 128/2) and its column in [q * 256 - 128/2, (q + 1) * 256 - 128/2).
All inputs are finite; a program needn't handle non-finite values.
Results may differ from a plain program's by a relative error of at most 0.0003.
Values sent between devices are 32-bit elements; how exact they have to be, the bound alone decides.
No kernel may reach another device: no remote copies, remote signals or barrier semaphores. Data moves between devices by JAX's collectives and lax.ppermute only.
A program may use at most 64 MiB of HBM per device.

v0:
```python
import math
import jax
import jax.numpy as jnp
from jax import lax
from jax.sharding import PartitionSpec as P

highest_mode = lax.Precision.HIGHEST


def from_behind(value, axis, steps):
    count = lax.axis_size(axis)
    first, last = (max(0, -steps), min(count, count - steps))
    return lax.ppermute(value, axis, [(source, source + steps) for source in range(first, last)])


def with_halo(array, sides, width):
    for axis, dim in sides:
        devices, length = (lax.axis_size(axis), array.shape[dim])
        up = [(i, (i + 1) % devices) for i in range(devices - 1)]
        down = [(j, i) for i, j in up]
        last = lax.slice_in_dim(array, length - width, length, axis=dim)
        first = lax.slice_in_dim(array, 0, width, axis=dim)
        before = lax.ppermute(last, axis, up)
        after = lax.ppermute(first, axis, down)
        array = jnp.concatenate([before, array, after], axis=dim)
    return array


def einsum_exact(form, first, second):
    return jnp.einsum(form, first, second, precision=highest_mode)


def make_tables(taps, width):
    reach = taps.shape[1] // 2
    pixel_idx = lax.iota(jnp.int32, width)
    offset = pixel_idx[None, :] - pixel_idx[:, None] + reach
    tap_idx = lax.iota(jnp.int32, taps.shape[1])
    one_hot = (offset[:, :, None] == tap_idx[None, None, :]).astype(jnp.float32)
    band_re = einsum_exact("abt,t->ab", one_hot, taps[0])
    band_im = einsum_exact("abt,t->ab", one_hot, taps[1])
    phase_idx = pixel_idx[:, None] * pixel_idx[None, :] % width
    angle = 2.0 * math.pi / width * phase_idx.astype(jnp.float32)
    norm_factor = 1.0 / math.sqrt(width)
    return (band_re, band_im, jnp.cos(angle) * norm_factor, -jnp.sin(angle) * norm_factor)


def both_sides(mat_re, mat_im, wave_re, wave_im):
    left_re = einsum_exact("ab,kbc->kac", mat_re, wave_re) - einsum_exact(
        "ab,kbc->kac", mat_im, wave_im
    )
    left_im = einsum_exact("ab,kbc->kac", mat_re, wave_im) + einsum_exact(
        "ab,kbc->kac", mat_im, wave_re
    )
    out_re = einsum_exact("kac,dc->kad", left_re, mat_re) - einsum_exact(
        "kac,dc->kad", left_im, mat_im
    )
    out_im = einsum_exact("kac,dc->kad", left_re, mat_im) + einsum_exact(
        "kac,dc->kad", left_im, mat_re
    )
    return (out_re, out_im)


def record_loss(probe, patch, measured_one, tables):
    band_re, band_im, dft_re, dft_im = tables
    wave_re = probe[:, 0]
    wave_im = probe[:, 1]
    layers = patch.shape[0]
    for layer_idx in range(layers):
        obj_re = patch[layer_idx, 0]
        obj_im = patch[layer_idx, 1]
        wave_re, wave_im = (
            wave_re * obj_re - wave_im * obj_im,
            wave_re * obj_im + wave_im * obj_re,
        )
        if layer_idx + 1 < layers:
            wave_re, wave_im = both_sides(band_re, band_im, wave_re, wave_im)
    far_re, far_im = both_sides(dft_re, dft_im, wave_re, wave_im)
    intensity = jnp.sum(far_re * far_re + far_im * far_im, axis=0)
    weight = 1.0 / (8.0 * probe.shape[0])
    return 0.5 * weight * jnp.sum((intensity - measured_one) ** 2)


def accumulate(grid, probe, measured, places, tables, patch_width):
    sizes = (grid.shape[0], 2, patch_width, patch_width)

    def one_record(carry, item):
        grad_grid, grad_probe = carry
        place, measured_one = item
        zero_idx = jnp.zeros((), jnp.int32)
        starts = (zero_idx, zero_idx, place[0], place[1])
        patch = lax.dynamic_slice(grid, starts, sizes)
        grad_wave, grad_patch = jax.grad(record_loss, argnums=(0, 1))(
            probe, patch, measured_one, tables
        )
        current = lax.dynamic_slice(grad_grid, starts, sizes)
        grad_grid = lax.dynamic_update_slice(grad_grid, current + grad_patch, starts)
        return ((grad_grid, grad_probe + grad_wave), None)

    init = (jnp.zeros(grid.shape, jnp.float32), jnp.zeros(probe.shape, jnp.float32))
    (grad_grid, grad_probe), unused = lax.scan(one_record, init, (places, measured))
    return (grad_grid, grad_probe)


def gram_of(first, second):
    stacked = jnp.concatenate([first, second], axis=0)
    col_re = stacked[:, 0]
    col_im = stacked[:, 1]
    gram_re = einsum_exact("ax,bx->ab", col_re, col_re) + einsum_exact("ax,bx->ab", col_im, col_im)
    gram_im = einsum_exact("ax,bx->ab", col_re, col_im) - einsum_exact("ax,bx->ab", col_im, col_re)
    return (gram_re, gram_im)


def complex_cholesky(herm_re, herm_im):
    count = herm_re.shape[0]
    order_idx = lax.iota(jnp.int32, count)
    cols_re = []
    cols_im = []
    for col_idx in range(count):
        numer_re = herm_re[:, col_idx]
        numer_im = herm_im[:, col_idx]
        for prev_idx in range(col_idx):
            vec_re = cols_re[prev_idx]
            vec_im = cols_im[prev_idx]
            pivot_re = vec_re[col_idx]
            pivot_im = vec_im[col_idx]
            numer_re = numer_re - (vec_re * pivot_re + vec_im * pivot_im)
            numer_im = numer_im - (vec_im * pivot_re - vec_re * pivot_im)
        diag_val = jnp.sqrt(numer_re[col_idx])
        below = order_idx > col_idx
        at_diag = order_idx == col_idx
        cols_re.append(
            jnp.where(below, numer_re / diag_val, 0.0) + jnp.where(at_diag, diag_val, 0.0)
        )
        cols_im.append(jnp.where(below, numer_im / diag_val, 0.0))
    return (jnp.stack(cols_re, axis=1), jnp.stack(cols_im, axis=1))


def lower_inverse(low_re, low_im):
    count = low_re.shape[0]
    unit = jnp.eye(count, dtype=low_re.dtype)
    rows_re = []
    rows_im = []
    for row_idx in range(count):
        acc_re = unit[row_idx]
        acc_im = jnp.zeros_like(unit[row_idx])
        for prev_idx in range(row_idx):
            coef_re = low_re[row_idx, prev_idx]
            coef_im = low_im[row_idx, prev_idx]
            acc_re = acc_re - (coef_re * rows_re[prev_idx] - coef_im * rows_im[prev_idx])
            acc_im = acc_im - (coef_re * rows_im[prev_idx] + coef_im * rows_re[prev_idx])
        rows_re.append(acc_re / low_re[row_idx, row_idx])
        rows_im.append(acc_im / low_re[row_idx, row_idx])
    return (jnp.stack(rows_re, axis=0), jnp.stack(rows_im, axis=0))


def orthonormalize(probe_cols, grad_cols, gram_re, gram_im, scale_out):
    modes = probe_cols.shape[0]
    trace_pp = jnp.trace(gram_re[:modes, :modes])
    trace_gg = jnp.trace(gram_re[modes:, modes:])
    factor = 0.5 * jnp.sqrt(trace_pp / (trace_gg + 1e-06))
    new_re = (
        gram_re[:modes, :modes]
        - factor * (gram_re[:modes, modes:] + gram_re[modes:, :modes])
        + factor * factor * gram_re[modes:, modes:]
    )
    new_im = (
        gram_im[:modes, :modes]
        - factor * (gram_im[:modes, modes:] + gram_im[modes:, :modes])
        + factor * factor * gram_im[modes:, modes:]
    )
    low_re, low_im = complex_cholesky(new_re, new_im)
    inv_re, inv_im = lower_inverse(low_re, low_im)
    right_re = inv_re.T
    right_im = -inv_im.T
    moved = probe_cols - factor * grad_cols
    moved_re = moved[:, 0]
    moved_im = moved[:, 1]
    out_re = einsum_exact("kx,kj->jx", moved_re, right_re) - einsum_exact(
        "kx,kj->jx", moved_im, right_im
    )
    out_im = einsum_exact("kx,kj->jx", moved_re, right_im) + einsum_exact(
        "kx,kj->jx", moved_im, right_re
    )
    return jnp.stack([out_re, out_im], axis=1) * scale_out


def fold_axis(grad, dim, half):
    full = grad.shape[dim]
    inner = full - 2 * half
    core = lax.slice_in_dim(grad, half, half + inner, axis=dim)
    for step_by in (1, -1):
        if step_by == 1:
            sent = lax.slice_in_dim(grad, half + inner, full, axis=dim)
        else:
            sent = lax.slice_in_dim(grad, 0, half, axis=dim)
        if dim == 2:
            arrived = from_behind(sent, "row", step_by)
        else:
            arrived = from_behind(sent, "col", step_by)
        widths = [(0, 0)] * grad.ndim
        if step_by == 1:
            widths[dim] = (0, inner - half)
        else:
            widths[dim] = (inner - half, 0)
        core = core + jnp.pad(arrived, widths)
    return core


def per_device(object_slices, probe, taps, measured, positions):
    width = probe.shape[-1]
    half = width // 2
    tile_rows = object_slices.shape[2]
    tile_cols = object_slices.shape[3]
    tables = make_tables(taps, width)
    extended = with_halo(object_slices, (("row", 2), ("col", 3)), half)
    anchor = jnp.stack(
        [lax.axis_index("row") * tile_rows - half, lax.axis_index("col") * tile_cols - half]
    )
    places = positions - anchor[None, :]
    grad_ext, grad_probe = accumulate(extended, probe, measured, places, tables, width)
    folded = fold_axis(fold_axis(grad_ext, 2, half), 3, half)
    modes = probe.shape[0]
    pixels = width * width
    probe_cols = probe.reshape(modes, 2, pixels)
    grad_cols = grad_probe.reshape(modes, 2, pixels)
    share = pixels // (lax.axis_size("row") * lax.axis_size("col"))
    start = lax.axis_index(("row", "col")) * share
    own_probe = lax.dynamic_slice_in_dim(probe_cols, start, share, 2)
    total_grad = lax.psum(grad_cols, ("row", "col"))
    gram_re, gram_im = gram_of(probe_cols, total_grad)
    own_grad = lax.dynamic_slice_in_dim(total_grad, start, share, 2)
    new_probe = orthonormalize(own_probe, own_grad, gram_re, gram_im, float(width))
    return (folded, new_probe)


def solution(mesh):
    placed = (
        P(None, None, ("groups", "row"), "col"),
        P("groups", None, None, None),
        P(),
        P(("groups", "row", "col"), None, None),
        P(("groups", "row", "col"), None),
    )
    return jax.shard_map(
        per_device,
        mesh=mesh,
        in_specs=placed,
        out_specs=(P(None, None, ("groups", "row"), "col"), P("groups", None, ("row", "col"))),
        check_vma=False,
    )
```

profile of v0, /device:TPU:0, one launch (start us, length us, event | category | flops | bytes accessed | tf_op | source)
XLA Modules:
  0.0 651.3 jit_solution(16764180511014686650)
XLA Ops:
  8.5 4.9 collective-permute-start
  16.4 1.6 iota_compare_fusion
  18.0 17.8 %collective-permute-done = f32[4,2,64,256]{3,2,1,0:T(8,128)S(1)} collective-permute-done((f32[4,2,64,256]{3,2,1,0:T(8,128)S(1)}, f32[4,2,64,256]{3,2,1,0:T(8,128)S(1)}, u32[]{:S(2)}, u32[]{:S(2)}) %collective-permute-start) | collective-permute-done | bytes 524320 | tf_op jit(solution)/shard_map/ppermute | solution.py:23
  39.0 2.1 collective-permute-start.2
  44.0 3.3 fusion.235
  47.3 3.2 fusion.233
  50.5 3.8 pad_maximum_fusion
  54.3 1.9 broadcast_in_dim.114
  56.2 173.7 %while.16 = (s32[]{:T(128)}, f32[4,2,256,384]{3,2,1,0:T(8,128)}, f32[8,2,128,128]{2,3,0,1:T(8,128)}, s32[2,2]{1,0:T(2,128)S(1)}, f32[8,2,128,128]{2,3,0,1:T(8,12...) while((s32[]{:T(128)}, f32[4,2,256,384]{3,2,1,0:T(8,128)}, ...), condition=%wide.region_18.19_spmd.clone.clone, body=%wide.region_0.18_spmd.clone.clone.sunk | while | flops 12914802688 | bytes 137233312 | solution.py:100
  61.4 2.2 constant_dynamic-slice_fusion.7
  87.5 1.6 copy.428
  90.6 2.3 fusion.624
  92.9 2.1 fusion.625
  108.3 1.7 multiply_reduce_fusion.15
  131.2 7.7 %dynamic_update_slice.9 = f32[4,2,256,384]{3,2,1,0:T(8,128)} dynamic-update-slice(f32[4,2,256,384]{3,2,1,0:T(8,128)} %get-tuple-element.615, f32[4,2,128,128]{3,2,1,0:T(8,128)S(1)} %add_add_fusion.2, s32[]{:T(128)} %constant.94.clone.1..sunk, s32[]{:T(128)} %constant.94.clone.1..sunk, s32[]{:T(128)S(6)} %select_n.471, s32[]{:T(128)S(6)} %select_n.472) | dynamic-update-slice | bytes 1048580 | tf_op jit(solution)/shard_map/while/body/eval_jaxpr/dynamic_update_slice | solution.py:96
  143.8 2.2 constant_dynamic-slice_fusion.7
  173.3 2.3 fusion.624
  175.6 2.1 fusion.625
  190.8 1.7 multiply_reduce_fusion.15
  210.7 2.4 select_add_fusion.2
  215.2 7.2 %dynamic_update_slice.9 = f32[4,2,256,384]{3,2,1,0:T(8,128)} dynamic-update-slice(f32[4,2,256,384]{3,2,1,0:T(8,128)} %get-tuple-element.615, f32[4,2,128,128]{3,2,1,0:T(8,128)S(1)} %add_add_fusion.2, s32[]{:T(128)} %constant.94.clone.1..sunk, s32[]{:T(128)} %constant.94.clone.1..sunk, s32[]{:T(128)S(6)} %select_n.471, s32[]{:T(128)S(6)} %select_n.472) | dynamic-update-slice | bytes 1048580 | tf_op jit(solution)/shard_map/while/body/eval_jaxpr/dynamic_update_slice | solution.py:96
  230.0 1.6 copy.336
  233.4 2.7 fusion.298
  236.1 5.0 collective-permute-start.4
  242.4 91.3 %all-reduce.16.cloned.1.call-done = f32[8,2,16384]{2,0,1:T(8,128)} async-done(((f32[8,2,16384]{2,0,1:T(8,128)}), f32[8,2,16384]{2,0,1:T(8,128)}) %all-reduce.16.cloned.1.call-update) | async-done | bytes 1048592 | tf_op jit(solution)/shard_map/psum | solution.py:229
  333.7 2.7 fusion.295
  336.4 2.7 convolution_add_fusion.25
  355.0 2.3 fusion.288
  358.6 2.3 compare_select_fusion.17
  363.4 3.8 fusion.286
  368.6 3.8 compare_select_fusion.15
  375.1 5.0 fusion.282
  381.5 5.1 compare_select_fusion.13
  389.2 6.2 add_subtract_fusion.2
  396.6 6.2 compare_select_fusion.11
  405.3 7.6 %add_subtract_fusion.1 = f32[8]{0:T(128)S(1)} fusion(f32[8]{0:T(128)S(1)} %compare_select_fusion.11, f32[8]{0:T(128)S(1)} %compare_select_fusion.13, f32[8]{0:T(128)S(1)} %compare_select_fusion.15, f32[8]{0:T(128)S(1)} %compare_select_fusion.17, f32[8]{0:T(128)S(1)} %compare_select_fusion.19, f32[8]{0:T(128)S(1)} %get-tuple-element.459, ...), kind=kLoop, calls=%fused_computation.455 | loop fusion | flops 432 | bytes 516 | tf_op jit(solution)/shard_map/sub | solution.py:126
  414.2 7.6 %compare_select_fusion.9 = f32[8]{0:T(128)S(1)} fusion(f32[8]{0:T(128)S(1)} %compare_select_fusion.11, f32[8]{0:T(128)S(1)} %compare_select_fusion.13, f32[8]{0:T(128)S(1)} %compare_select_fusion.15, f32[8]{0:T(128)S(1)} %compare_select_fusion.17, f32[8]{0:T(128)S(1)} %compare_select_fusion.19, f32[8]{0:T(128)S(1)} %get-tuple-element.460, ...), kind=kLoop, calls=%fused_computation.391 | loop fusion | flops 456 | bytes 520 | tf_op jit(solution)/shard_map/jit(_where)/select_n | solution.py:134
  423.6 8.8 %add_subtract_fusion = f32[8]{0:T(128)S(1)} fusion(f32[8]{0:T(128)S(1)} %compare_select_fusion.9, f32[8]{0:T(128)S(1)} %compare_select_fusion.11, f32[8]{0:T(128)S(1)} %compare_select_fusion.13, f32[8]{0:T(128)S(1)} %compare_select_fusion.15, f32[8]{0:T(128)S(1)} %compare_select_fusion.17, f32[8]{0:T(128)S(1)} %compare_select_fusion.19, ...), kind=kLoop, calls=%fused_computation.454 | loop fusion | flops 512 | bytes 592 | tf_op jit(solution)/shard_map/sub | solution.py:126
  434.1 39.2 %subtract_divide_fusion.1 = (f32[1,8]{0,1:T(8,128)S(1)}, f32[1,8]{0,1:T(8,128)S(1)}, f32[1,8]{0,1:T(8,128)S(1)}, f32[1,8]{0,1:T(8,128)S(1)}, f32[1,8]{0,1:T(8,128)S(1)}) fusion(f32[8,8]{0,1:T(8,128)S(1)} %fusion.251, f32[]{:T(128)} %bitcast.99, f32[]{:T(128)} %bitcast.67, f32[]{:T(128)S(6)} %mul.2504, f32[]{:T(128)} %bitcast.96, f32[]{:T(128)} %bitcast.94, ...), kind=kLoop, calls=%fused_computation.360 | loop fusion | flops 1576 | bytes 720 | tf_op jit(solution)/shard_map/div | solution.py:151
  473.4 27.4 %subtract_divide_fusion.3 = f32[1,8]{0,1:T(8,128)S(1)} fusion(f32[]{:T(128)} %bitcast.81, f32[1,8]{0,1:T(8,128)S(1)} %get-tuple-element.353, f32[1,8]{0,1:T(8,128)S(1)} %get-tuple-element.354, f32[1,8]{0,1:T(8,128)S(1)} %get-tuple-element.355, f32[1,8]{0,1:T(8,128)S(1)} %get-tuple-element.356, f32[]{:T(128)} %bitcast.53, f32[8,8]{0,1:T(8,128)S(1)} %fusion.251, ...), kind=kLoop, calls=%fused_computation.362 | loop fusion | flops 960 | bytes 464 | tf_op jit(solution)/shard_map/div | solution.py:151
  500.8 19.0 %subtract_divide_fusion.5 = f32[1,8]{0,1:T(8,128)S(1)} fusion(f32[1,8]{0,1:T(8,128)S(1)} %get-tuple-element.354, f32[1,8]{0,1:T(8,128)S(1)} %get-tuple-element.355, f32[1,8]{0,1:T(8,128)S(1)} %get-tuple-element.356, f32[1,8]{0,1:T(8,128)S(1)} %get-tuple-element.353, f32[8,8]{0,1:T(8,128)S(1)} %fusion.251, f32[]{:T(128)} %bitcast.65, f32[]{:T(128)} %bitcast.41, ...), kind=kLoop, calls=%fused_computation.365 | loop fusion | flops 608 | bytes 372 | tf_op jit(solution)/shard_map/div | solution.py:151
  519.8 12.3 %subtract_divide_fusion.7 = f32[1,8]{0,1:T(8,128)S(1)} fusion(f32[1,8]{0,1:T(8,128)S(1)} %get-tuple-element.353, f32[1,8]{0,1:T(8,128)S(1)} %get-tuple-element.354, f32[1,8]{0,1:T(8,128)S(1)} %get-tuple-element.355, f32[1,8]{0,1:T(8,128)S(1)} %get-tuple-element.356, f32[8,8]{0,1:T(8,128)S(1)} %fusion.251, f32[]{:T(128)} %bitcast.51, f32[]{:T(128)} %bitcast.31, ...), kind=kLoop, calls=%fused_computation.368 | loop fusion | flops 320 | bytes 288 | tf_op jit(solution)/shard_map/div | solution.py:151
  532.7 27.3 %subtract_divide_fusion.2 = f32[1,8]{0,1:T(8,128)S(1)} fusion(f32[1,8]{0,1:T(8,128)S(1)} %get-tuple-element.353, f32[1,8]{0,1:T(8,128)S(1)} %get-tuple-element.354, f32[1,8]{0,1:T(8,128)S(1)} %get-tuple-element.355, f32[1,8]{0,1:T(8,128)S(1)} %get-tuple-element.356, f32[]{:T(128)} %bitcast.67, f32[]{:T(128)S(6)} %mul.2504, f32[]{:T(128)} %bitcast.81, ...), kind=kLoop, calls=%fused_computation.361 | loop fusion | flops 960 | bytes 432 | tf_op jit(solution)/shard_map/div | solution.py:152
  559.9 19.0 %subtract_divide_fusion.4 = f32[1,8]{0,1:T(8,128)S(1)} fusion(f32[1,8]{0,1:T(8,128)S(1)} %get-tuple-element.353, f32[1,8]{0,1:T(8,128)S(1)} %get-tuple-element.354, f32[1,8]{0,1:T(8,128)S(1)} %get-tuple-element.355, f32[1,8]{0,1:T(8,128)S(1)} %get-tuple-element.356, f32[]{:T(128)} %bitcast.53, f32[]{:T(128)S(6)} %mul.2430, f32[]{:T(128)} %bitcast.65, ...), kind=kLoop, calls=%fused_computation.363 | loop fusion | flops 608 | bytes 340 | tf_op jit(solution)/shard_map/div | solution.py:152
  578.9 7.2 %subtract_divide_fusion.8 = (f32[1,8]{0,1:T(8,128)S(1)}, f32[1,8]{0,1:T(8,128)S(1)}, f32[1,8]{0,1:T(8,128)S(1)}) fusion(f32[1,8]{0,1:T(8,128)S(1)} %get-tuple-element.354, f32[1,8]{0,1:T(8,128)S(1)} %get-tuple-element.355, f32[1,8]{0,1:T(8,128)S(1)} %get-tuple-element.356, f32[]{:T(128)} %bitcast.31, f32[]{:T(128)S(6)} %mul.2318, f32[]{:T(128)} %bitcast.39, ...), kind=kLoop, calls=%fused_computation.369 | loop fusion | flops 192 | bytes 252 | tf_op jit(solution)/shard_map/div | solution.py:152
  586.1 36.6 %subtract_divide_fusion = f32[1,8]{0,1:T(8,128)S(1)} fusion(f32[1,8]{0,1:T(8,128)S(1)} %get-tuple-element.353, f32[1,8]{0,1:T(8,128)S(1)} %get-tuple-element.354, f32[1,8]{0,1:T(8,128)S(1)} %get-tuple-element.355, f32[1,8]{0,1:T(8,128)S(1)} %get-tuple-element.356, f32[]{:T(128)} %bitcast.83, f32[]{:T(128)S(6)} %mul.2550, f32[]{:T(128)} %bitcast.99, ...), kind=kLoop, calls=%fused_computation.359 | loop fusion | flops 1376 | bytes 532 | tf_op jit(solution)/shard_map/div | solution.py:152
  622.8 12.2 %subtract_divide_fusion.6 = f32[1,8]{0,1:T(8,128)S(1)} fusion(f32[1,8]{0,1:T(8,128)S(1)} %get-tuple-element.353, f32[1,8]{0,1:T(8,128)S(1)} %get-tuple-element.354, f32[1,8]{0,1:T(8,128)S(1)} %get-tuple-element.355, f32[1,8]{0,1:T(8,128)S(1)} %get-tuple-element.356, f32[]{:T(128)} %bitcast.41, f32[]{:T(128)S(6)} %mul.2368, f32[]{:T(128)} %bitcast.51, ...), kind=kLoop, calls=%fused_computation.366 | loop fusion | flops 320 | bytes 256 | tf_op jit(solution)/shard_map/div | solution.py:152
  635.6 1.9 pad_add_fusion
  (323 shorter events, 162.1 us)
Async XLA Ops:
  7.2 326.5 %all-reduce.16.cloned.1.call-start = ((), (), s32[]{:S(2)}) async-start(), calls=%async_computation | async-start | bytes 2097152 | tf_op jit(solution)/shard_map/psum | solution.py:229
  8.5 27.2 %collective-permute-start = (f32[4,2,64,256]{3,2,1,0:T(8,128)S(1)}, f32[4,2,64,256]{3,2,1,0:T(8,128)S(1)}, u32[]{:S(2)}, u32[]{:S(2)}) collective-permute-start(f32[4,2,64,256]{3,2,1,0:T(8,128)S(1)} %get-tuple-element.392), channel_id=1, source_target_pairs={{0,2},{2,4},{4,6},{6,8},{8,10},{10,12},{12,14},{1,3},{3,5},{5,7},{... | collective-permute-start | bytes 1572872 | tf_op jit(solution)/shard_map/ppermute | solution.py:23
  13.4 22.7 %collective-permute-start.1 = (f32[4,2,64,256]{3,2,1,0:T(8,128)S(1)}, f32[4,2,64,256]{3,2,1,0:T(8,128)}, u32[]{:S(2)}, u32[]{:S(2)}) collective-permute-start(f32[4,2,64,256]{3,2,1,0:T(8,128)S(1)} %get-tuple-element.393), channel_id=1, source_target_pairs={{2,0},{4,2},{6,4},{8,6},{10,8},{12,10},{14,12},{3,1},{5,3},{7,5},{... | collective-permute-start | bytes 1572872 | tf_op jit(solution)/shard_map/ppermute | solution.py:24
  36.1 6.2 copy-start.23
  37.5 4.9 copy-start.9
  37.5 6.4 copy-start.24
  39.0 11.5 %collective-permute-start.2 = (f32[4,2,256,64]{2,3,1,0:T(8,128)}, f32[4,2,256,64]{2,3,1,0:T(8,128)}, u32[]{:S(2)}, u32[]{:S(2)}) collective-permute-start(f32[4,2,256,64]{2,3,1,0:T(8,128)} %get-tuple-element.388), channel_id=1, source_target_pairs={{0,1},{2,3},{4,5},{6,7},{8,9},{10,11},{12,13},{14,15},{16,17},{18,... | collective-permute-start | bytes 1572872 | tf_op jit(solution)/shard_map/ppermute | solution.py:23
  41.1 9.5 %collective-permute-start.3 = (f32[4,2,256,64]{2,3,1,0:T(8,128)}, f32[4,2,256,64]{2,3,1,0:T(8,128)}, u32[]{:S(2)}, u32[]{:S(2)}) collective-permute-start(f32[4,2,256,64]{2,3,1,0:T(8,128)} %get-tuple-element.389), channel_id=1, source_target_pairs={{1,0},{3,2},{5,4},{7,6},{9,8},{11,10},{13,12},{15,14},{17,16},{19,... | collective-permute-start | bytes 1572872 | tf_op jit(solution)/shard_map/ppermute | solution.py:24
  44.0 6.6 %copy-start.10 = (f32[4,2,64,256]{2,3,1,0:T(8,128)S(1)}, f32[4,2,64,256]{2,3,1,0:T(8,128)}, u32[]{:S(2)}) copy-start(f32[4,2,64,256]{2,3,1,0:T(8,128)} %copy-done.9) | copy-start | bytes 1572868
  56.7 9.2 %copy-start = (f32[8,2,128,128]{2,3,0,1:T(8,128)}, f32[8,2,128,128]{2,3,0,1:T(8,128)S(1)}, u32[]{:S(2)}) copy-start(f32[8,2,128,128]{2,3,0,1:T(8,128)S(1)} %get-tuple-element.634) | copy-start | bytes 3145732 | tf_op jit(solution)/shard_map/while
  63.6 3.4 copy-start.4
  63.6 3.4 copy-start.6
  90.6 4.4 copy-start.2
  90.6 4.4 copy-start.3
  97.4 4.5 copy-start.22
  123.2 3.6 copy-start.5
  123.2 3.6 copy-start.7
  123.8 3.0 copy-start.1
  126.8 2.3 copy-start.11
  126.9 2.3 copy-start.12
  126.9 2.3 copy-start.13
  126.9 2.3 copy-start.14
  128.0 1.2 copy-start.15
  139.2 9.2 %copy-start = (f32[8,2,128,128]{2,3,0,1:T(8,128)}, f32[8,2,128,128]{2,3,0,1:T(8,128)S(1)}, u32[]{:S(2)}) copy-start(f32[8,2,128,128]{2,3,0,1:T(8,128)S(1)} %get-tuple-element.634) | copy-start | bytes 3145732 | tf_op jit(solution)/shard_map/while
  146.0 3.4 copy-start.4
  146.0 3.4 copy-start.6
  173.3 4.4 copy-start.2
  173.3 4.4 copy-start.3
  180.0 4.5 copy-start.22
  205.9 3.6 copy-start.5
  205.9 3.6 copy-start.7
  206.5 3.0 copy-start.1
  209.5 3.7 copy-start.11
  209.5 3.7 copy-start.12
  209.6 3.7 copy-start.13
  209.6 3.7 copy-start.14
  210.7 2.5 copy-start.17
  210.7 2.5 copy-start.18
  210.7 2.5 copy-start.19
  210.7 2.5 copy-start.20
  210.7 2.6 copy-start.15
  210.7 2.6 copy-start.16
  229.9 2.9 copy-start.21
  236.1 399.5 %collective-permute-start.4 = (f32[4,2,64,384]{3,2,1,0:T(8,128)}, f32[4,2,64,384]{3,2,1,0:T(8,128)S(1)}, u32[]{:S(2)}, u32[]{:S(2)}) collective-permute-start(f32[4,2,64,384]{3,2,1,0:T(8,128)} %get-tuple-element.386), channel_id=1, source_target_pairs={{0,2},{2,4},{4,6},{6,8},{8,10},{10,12},{12,14},{1,3},{3,5},{5,7},{... | collective-permute-start | bytes 2359304 | tf_op jit(solution)/shard_map/ppermute | solution.py:13
  241.1 394.5 %collective-permute-start.5 = (f32[4,2,64,384]{3,2,1,0:T(8,128)}, f32[4,2,64,384]{3,2,1,0:T(8,128)}, u32[]{:S(2)}, u32[]{:S(2)}) collective-permute-start(f32[4,2,64,384]{3,2,1,0:T(8,128)} %get-tuple-element.387), channel_id=1, source_target_pairs={{2,0},{4,2},{6,4},{8,6},{10,8},{12,10},{14,12},{3,1},{5,3},{7,5},{... | collective-permute-start | bytes 2359304 | tf_op jit(solution)/shard_map/ppermute | solution.py:13
  333.7 8.8 %copy-start.8 = (f32[8,2,16384]{2,0,1:T(8,128)S(1)}, f32[8,2,16384]{2,0,1:T(8,128)}, u32[]{:S(2)}) copy-start(f32[8,2,16384]{2,0,1:T(8,128)} %all-reduce.16.cloned.1.call-done) | copy-start | bytes 3145732
  637.7 3.8 collective-permute-start.6
  639.0 3.8 collective-permute-start.7
  (5 other events, 5.9 us)
Sparse Core Ops, SparseCore 0:
  232.9 100.7 all-reduce.15
where the time goes:
time: 663 us; the launch traced here: 651 us
  other arithmetic  279 us (42%)
  matrix products  135 us (20%)
  waiting for transfers between devices  110 us (17%)
  local copies, waits for them, and re-layouts  59.8 us (9%)
  between operations  30.9 us (5%)
  starting transfers between devices  18.4 us (3%)
  loops' own time  17.8 us (3%)
    dot_general x138, matrix products, einsum_exact(): return jnp.einsum(form, first, second, precision=highest_mode)  135 us
    div x5, other arithmetic, lower_inverse(): rows_im.append(acc_im / low_re[row_idx, row_idx])  102 us
    div x4, other arithmetic, lower_inverse(): rows_re.append(acc_re / low_re[row_idx, row_idx])  97.9 us
    psum x1, waiting for transfers between devices, per_device(): total_grad = lax.psum(grad_cols, ('row', 'col'))  91.3 us
    sub x7, other arithmetic, complex_cholesky(): numer_re = numer_re - (vec_re * pivot_re + vec_im * pivot_im)  34.9 us
    select_n x7, other arithmetic, complex_cholesky(): cols_im.append(jnp.where(below, numer_im / diag_val, 0.0))  26.1 us
    another operation x1, loops' own time, accumulate(): lax.scan(one_record, init, (places, measured))  17.8 us
    ppermute x2, waiting for transfers between devices, with_halo(): before = lax.ppermute(last, axis, up)  17.8 us
  transfers between devices with their start and end apart: 9, of which 3 were waited for; matrix products, arithmetic and copies ran while one was open for 46% of the time, Pallas kernels for 0%

commit v1 on v0

--- a/solution.py
+++ b/solution.py
@@ -1,3 +1,4 @@
+import functools
 import math
 import jax
 import jax.numpy as jnp
@@ -5,6 +6,14 @@
 from jax.sharding import PartitionSpec as P
 
 highest_mode = lax.Precision.HIGHEST
+
+
+def store_the_shelves(sheet, named_axis, dev_axis):
+    w1 = lax.psum(lax.psum(sheet, named_axis), dev_axis)
+    return w1
+
+
+match_vectors_on_mesh = functools.partial(store_the_shelves, named_axis="col", dev_axis="row")
 
 
 def from_behind(value, axis, steps):
@@ -226,7 +235,7 @@
     share = pixels // (lax.axis_size("row") * lax.axis_size("col"))
     start = lax.axis_index(("row", "col")) * share
     own_probe = lax.dynamic_slice_in_dim(probe_cols, start, share, 2)
-    total_grad = lax.psum(grad_cols, ("row", "col"))
+    total_grad = match_vectors_on_mesh(grad_cols)
     gram_re, gram_im = gram_of(probe_cols, total_grad)
     own_grad = lax.dynamic_slice_in_dim(total_grad, start, share, 2)
     new_probe = orthonormalize(own_probe, own_grad, gram_re, gram_im, float(width))

time: 663 us -> 668 us (level)
    psum x1 -> x2, waiting for transfers between devices: 91.3 us -> 70.9 us  [store_the_shelves(): w1 = lax.psum(lax.psum(sheet, named_axis), dev_axis)]
    ppermute x4, waiting for transfers between devices: 1.35 us -> 21.8 us  [from_behind(): lax.ppermute(value, axis, [(source, source + steps) for source in range(f...]
  transfers between devices with their start and end apart: 9 -> 10, of which waited for: 3 -> 5; matrix products, arithmetic and copies ran while one was open for 46% -> 3% of each run, Pallas kernels for 0% -> 0%
where the time goes in v1:
time: 668 us; the launch traced here: 656 us
  other arithmetic  281 us (42%)
  matrix products  135 us (20%)
  waiting for transfers between devices  110 us (16%)
  local copies, waits for them, and re-layouts  60.9 us (9%)
  between operations  30.9 us (5%)
  starting transfers between devices  20.9 us (3%)
  loops' own time  17.1 us (3%)
    dot_general x138, matrix products, einsum_exact(): return jnp.einsum(form, first, second, precision=highest_mode)  135 us
    div x5, other arithmetic, lower_inverse(): rows_im.append(acc_im / low_re[row_idx, row_idx])  103 us
    div x4, other arithmetic, lower_inverse(): rows_re.append(acc_re / low_re[row_idx, row_idx])  97.9 us
    psum x2, waiting for transfers between devices, store_the_shelves(): w1 = lax.psum(lax.psum(sheet, named_axis), dev_axis)  70.9 us
    sub x7, other arithmetic, complex_cholesky(): numer_re = numer_re - (vec_re * pivot_re + vec_im * pivot_im)  35.2 us
    select_n x7, other arithmetic, complex_cholesky(): cols_im.append(jnp.where(below, numer_im / diag_val, 0.0))  26.2 us
    ppermute x4, waiting for transfers between devices, from_behind(): lax.ppermute(value, axis, [(source, source + steps) for source in range(f...  21.8 us
    ppermute x2, waiting for transfers between devices, with_halo(): before = lax.ppermute(last, axis, up)  17.8 us
  transfers between devices with their start and end apart: 10, of which 5 were waited for; matrix products, arithmetic and copies ran while one was open for 3% of the time, Pallas kernels for 0%

profile of v1, /device:TPU:0, one launch (start us, length us, event | category | flops | bytes accessed | tf_op | source)
XLA Modules:
  0.0 656.3 jit_solution(12243490238859473198)
XLA Ops:
  8.5 4.9 collective-permute-start
  18.0 17.8 %collective-permute-done = f32[4,2,64,256]{3,2,1,0:T(8,128)S(1)} collective-permute-done((f32[4,2,64,256]{3,2,1,0:T(8,128)S(1)}, f32[4,2,64,256]{3,2,1,0:T(8,128)S(1)}, u32[]{:S(2)}, u32[]{:S(2)}) %collective-permute-start) | collective-permute-done | bytes 524320 | tf_op jit(solution)/shard_map/ppermute | solution.py:32
  39.0 2.1 collective-permute-start.2
  44.0 3.3 fusion.235
  47.3 3.2 fusion.233
  50.6 3.7 pad_maximum_fusion
  54.3 1.9 broadcast_in_dim.114
  56.2 172.9 %while.16 = (s32[]{:T(128)}, f32[4,2,256,384]{3,2,1,0:T(8,128)}, f32[8,2,128,128]{2,3,0,1:T(8,128)}, s32[2,2]{1,0:T(2,128)S(1)}, f32[8,2,128,128]{2,3,0,1:T(8,12...) while((s32[]{:T(128)}, f32[4,2,256,384]{3,2,1,0:T(8,128)}, ...), condition=%wide.region_18.19_spmd.clone.clone, body=%wide.region_0.18_spmd.clone.clone.sunk | while | flops 12914802688 | bytes 137233312 | solution.py:109
  61.0 2.2 constant_dynamic-slice_fusion.7
  90.2 2.3 fusion.624
  92.5 2.1 fusion.625
  130.8 7.7 %dynamic_update_slice.9 = f32[4,2,256,384]{3,2,1,0:T(8,128)} dynamic-update-slice(f32[4,2,256,384]{3,2,1,0:T(8,128)} %get-tuple-element.615, f32[4,2,128,128]{3,2,1,0:T(8,128)S(1)} %add_add_fusion.2, s32[]{:T(128)} %constant.94.clone.1..sunk, s32[]{:T(128)} %constant.94.clone.1..sunk, s32[]{:T(128)S(6)} %select_n.471, s32[]{:T(128)S(6)} %select_n.472) | dynamic-update-slice | bytes 1048580 | tf_op jit(solution)/shard_map/while/body/eval_jaxpr/dynamic_update_slice | solution.py:105
  143.0 2.2 constant_dynamic-slice_fusion.7
  172.5 2.3 fusion.624
  174.7 2.1 fusion.625
  209.9 2.4 select_add_fusion.2
  214.4 7.2 %dynamic_update_slice.9 = f32[4,2,256,384]{3,2,1,0:T(8,128)} dynamic-update-slice(f32[4,2,256,384]{3,2,1,0:T(8,128)} %get-tuple-element.615, f32[4,2,128,128]{3,2,1,0:T(8,128)S(1)} %add_add_fusion.2, s32[]{:T(128)} %constant.94.clone.1..sunk, s32[]{:T(128)} %constant.94.clone.1..sunk, s32[]{:T(128)S(6)} %select_n.471, s32[]{:T(128)S(6)} %select_n.472) | dynamic-update-slice | bytes 1048580 | tf_op jit(solution)/shard_map/while/body/eval_jaxpr/dynamic_update_slice | solution.py:105
  229.2 2.7 copy.336
  231.9 2.4 reshape.371
  235.6 5.9 collective-permute-start.4
  242.7 15.8 %all-reduce.17.cloned.1.call-done = f32[8,2,16384]{2,0,1:T(8,128)} async-done(((f32[8,2,16384]{2,0,1:T(8,128)}), f32[8,2,16384]{2,0,1:T(8,128)}) %all-reduce.17.cloned.1.call-update) | async-done | bytes 1048592 | tf_op jit(solution)/shard_map/psum | solution.py:12
  258.6 19.9 %collective-permute-done.4 = f32[4,2,64,384]{3,2,1,0:T(8,128)} collective-permute-done((f32[4,2,64,384]{3,2,1,0:T(8,128)}, f32[4,2,64,384]{3,2,1,0:T(8,128)}, u32[]{:S(2)}, u32[]{:S(2)}) %collective-permute-start.4) | collective-permute-done | bytes 786464 | tf_op jit(solution)/shard_map/ppermute | solution.py:22
  280.3 2.8 collective-permute-start.6
  285.1 1.8 collective-permute-done.7
  286.9 2.9 fusion.242
  289.8 55.0 %all-reduce.19.cloned.1.call-done = f32[8,2,16384]{2,0,1:T(8,128)} async-done(((f32[8,2,16384]{2,0,1:T(8,128)}), f32[8,2,16384]{2,0,1:T(8,128)}) %all-reduce.19.cloned.1.call-update) | async-done | bytes 1048592 | tf_op jit(solution)/shard_map/psum | solution.py:12
  344.9 2.7 fusion.295
  347.6 2.7 convolution_add_fusion.25
  366.4 2.5 fusion.288
  370.2 2.5 compare_select_fusion.17
  375.3 3.7 fusion.286
  380.2 3.7 compare_select_fusion.15
  386.4 4.9 fusion.282
  392.8 4.9 compare_select_fusion.13
  400.3 6.1 add_subtract_fusion.2
  407.5 6.1 compare_select_fusion.11
  416.2 7.7 %add_subtract_fusion.1 = f32[8]{0:T(128)S(1)} fusion(f32[8]{0:T(128)S(1)} %compare_select_fusion.11, f32[8]{0:T(128)S(1)} %compare_select_fusion.13, f32[8]{0:T(128)S(1)} %compare_select_fusion.15, f32[8]{0:T(128)S(1)} %compare_select_fusion.17, f32[8]{0:T(128)S(1)} %compare_select_fusion.19, f32[8]{0:T(128)S(1)} %get-tuple-element.459, ...), kind=kLoop, calls=%fused_computation.455 | loop fusion | flops 432 | bytes 516 | tf_op jit(solution)/shard_map/sub | solution.py:135
  425.3 7.7 %compare_select_fusion.9 = f32[8]{0:T(128)S(1)} fusion(f32[8]{0:T(128)S(1)} %compare_select_fusion.11, f32[8]{0:T(128)S(1)} %compare_select_fusion.13, f32[8]{0:T(128)S(1)} %compare_select_fusion.15, f32[8]{0:T(128)S(1)} %compare_select_fusion.17, f32[8]{0:T(128)S(1)} %compare_select_fusion.19, f32[8]{0:T(128)S(1)} %get-tuple-element.460, ...), kind=kLoop, calls=%fused_computation.391 | loop fusion | flops 456 | bytes 520 | tf_op jit(solution)/shard_map/jit(_where)/select_n | solution.py:143
  434.9 9.0 %add_subtract_fusion = f32[8]{0:T(128)S(1)} fusion(f32[8]{0:T(128)S(1)} %compare_select_fusion.9, f32[8]{0:T(128)S(1)} %compare_select_fusion.11, f32[8]{0:T(128)S(1)} %compare_select_fusion.13, f32[8]{0:T(128)S(1)} %compare_select_fusion.15, f32[8]{0:T(128)S(1)} %compare_select_fusion.17, f32[8]{0:T(128)S(1)} %compare_select_fusion.19, ...), kind=kLoop, calls=%fused_computation.454 | loop fusion | flops 512 | bytes 592 | tf_op jit(solution)/shard_map/sub | solution.py:135
  445.8 39.3 %subtract_divide_fusion.1 = (f32[1,8]{0,1:T(8,128)S(1)}, f32[1,8]{0,1:T(8,128)S(1)}, f32[1,8]{0,1:T(8,128)S(1)}, f32[1,8]{0,1:T(8,128)S(1)}, f32[1,8]{0,1:T(8,128)S(1)}) fusion(f32[8,8]{0,1:T(8,128)S(1)} %fusion.251, f32[]{:T(128)} %bitcast.99, f32[]{:T(128)} %bitcast.67, f32[]{:T(128)S(6)} %mul.2504, f32[]{:T(128)} %bitcast.96, f32[]{:T(128)} %bitcast.94, ...), kind=kLoop, calls=%fused_computation.360 | loop fusion | flops 1576 | bytes 720 | tf_op jit(solution)/shard_map/div | solution.py:160
  485.1 27.2 %subtract_divide_fusion.3 = f32[1,8]{0,1:T(8,128)S(1)} fusion(f32[]{:T(128)} %bitcast.81, f32[1,8]{0,1:T(8,128)S(1)} %get-tuple-element.353, f32[1,8]{0,1:T(8,128)S(1)} %get-tuple-element.354, f32[1,8]{0,1:T(8,128)S(1)} %get-tuple-element.355, f32[1,8]{0,1:T(8,128)S(1)} %get-tuple-element.356, f32[]{:T(128)} %bitcast.53, f32[8,8]{0,1:T(8,128)S(1)} %fusion.251, ...), kind=kLoop, calls=%fused_computation.362 | loop fusion | flops 960 | bytes 464 | tf_op jit(solution)/shard_map/div | solution.py:160
  512.3 19.1 %subtract_divide_fusion.5 = f32[1,8]{0,1:T(8,128)S(1)} fusion(f32[1,8]{0,1:T(8,128)S(1)} %get-tuple-element.354, f32[1,8]{0,1:T(8,128)S(1)} %get-tuple-element.355, f32[1,8]{0,1:T(8,128)S(1)} %get-tuple-element.356, f32[1,8]{0,1:T(8,128)S(1)} %get-tuple-element.353, f32[8,8]{0,1:T(8,128)S(1)} %fusion.251, f32[]{:T(128)} %bitcast.65, f32[]{:T(128)} %bitcast.41, ...), kind=kLoop, calls=%fused_computation.365 | loop fusion | flops 608 | bytes 372 | tf_op jit(solution)/shard_map/div | solution.py:160
  531.3 12.4 %subtract_divide_fusion.7 = f32[1,8]{0,1:T(8,128)S(1)} fusion(f32[1,8]{0,1:T(8,128)S(1)} %get-tuple-element.353, f32[1,8]{0,1:T(8,128)S(1)} %get-tuple-element.354, f32[1,8]{0,1:T(8,128)S(1)} %get-tuple-element.355, f32[1,8]{0,1:T(8,128)S(1)} %get-tuple-element.356, f32[8,8]{0,1:T(8,128)S(1)} %fusion.251, f32[]{:T(128)} %bitcast.51, f32[]{:T(128)} %bitcast.31, ...), kind=kLoop, calls=%fused_computation.368 | loop fusion | flops 320 | bytes 288 | tf_op jit(solution)/shard_map/div | solution.py:160
  544.4 27.3 %subtract_divide_fusion.2 = f32[1,8]{0,1:T(8,128)S(1)} fusion(f32[1,8]{0,1:T(8,128)S(1)} %get-tuple-element.353, f32[1,8]{0,1:T(8,128)S(1)} %get-tuple-element.354, f32[1,8]{0,1:T(8,128)S(1)} %get-tuple-element.355, f32[1,8]{0,1:T(8,128)S(1)} %get-tuple-element.356, f32[]{:T(128)} %bitcast.67, f32[]{:T(128)S(6)} %mul.2504, f32[]{:T(128)} %bitcast.81, ...), kind=kLoop, calls=%fused_computation.361 | loop fusion | flops 960 | bytes 432 | tf_op jit(solution)/shard_map/div | solution.py:161
  571.7 19.0 %subtract_divide_fusion.4 = f32[1,8]{0,1:T(8,128)S(1)} fusion(f32[1,8]{0,1:T(8,128)S(1)} %get-tuple-element.353, f32[1,8]{0,1:T(8,128)S(1)} %get-tuple-element.354, f32[1,8]{0,1:T(8,128)S(1)} %get-tuple-element.355, f32[1,8]{0,1:T(8,128)S(1)} %get-tuple-element.356, f32[]{:T(128)} %bitcast.53, f32[]{:T(128)S(6)} %mul.2430, f32[]{:T(128)} %bitcast.65, ...), kind=kLoop, calls=%fused_computation.363 | loop fusion | flops 608 | bytes 340 | tf_op jit(solution)/shard_map/div | solution.py:161
  590.7 12.4 %subtract_divide_fusion.6 = f32[1,8]{0,1:T(8,128)S(1)} fusion(f32[1,8]{0,1:T(8,128)S(1)} %get-tuple-element.353, f32[1,8]{0,1:T(8,128)S(1)} %get-tuple-element.354, f32[1,8]{0,1:T(8,128)S(1)} %get-tuple-element.355, f32[1,8]{0,1:T(8,128)S(1)} %get-tuple-element.356, f32[]{:T(128)} %bitcast.41, f32[]{:T(128)S(6)} %mul.2368, f32[]{:T(128)} %bitcast.51, ...), kind=kLoop, calls=%fused_computation.366 | loop fusion | flops 320 | bytes 256 | tf_op jit(solution)/shard_map/div | solution.py:161
  603.1 7.5 %subtract_divide_fusion.8 = (f32[1,8]{0,1:T(8,128)S(1)}, f32[1,8]{0,1:T(8,128)S(1)}, f32[1,8]{0,1:T(8,128)S(1)}) fusion(f32[1,8]{0,1:T(8,128)S(1)} %get-tuple-element.354, f32[1,8]{0,1:T(8,128)S(1)} %get-tuple-element.355, f32[1,8]{0,1:T(8,128)S(1)} %get-tuple-element.356, f32[]{:T(128)} %bitcast.31, f32[]{:T(128)S(6)} %mul.2318, f32[]{:T(128)} %bitcast.39, ...), kind=kLoop, calls=%fused_computation.369 | loop fusion | flops 192 | bytes 252 | tf_op jit(solution)/shard_map/div | solution.py:161
  610.6 36.9 %subtract_divide_fusion = f32[1,8]{0,1:T(8,128)S(1)} fusion(f32[1,8]{0,1:T(8,128)S(1)} %get-tuple-element.353, f32[1,8]{0,1:T(8,128)S(1)} %get-tuple-element.354, f32[1,8]{0,1:T(8,128)S(1)} %get-tuple-element.355, f32[1,8]{0,1:T(8,128)S(1)} %get-tuple-element.356, f32[]{:T(128)} %bitcast.83, f32[]{:T(128)S(6)} %mul.2550, f32[]{:T(128)} %bitcast.99, ...), kind=kLoop, calls=%fused_computation.359 | loop fusion | flops 1376 | bytes 532 | tf_op jit(solution)/shard_map/div | solution.py:161
  (330 shorter events, 166.5 us)
Async XLA Ops:
  7.2 251.4 %all-reduce.17.cloned.1.call-start = ((), (), s32[]{:S(2)}) async-start(), calls=%async_computation | async-start | bytes 2097152 | tf_op jit(solution)/shard_map/psum | solution.py:12
  8.5 27.2 %collective-permute-start = (f32[4,2,64,256]{3,2,1,0:T(8,128)S(1)}, f32[4,2,64,256]{3,2,1,0:T(8,128)S(1)}, u32[]{:S(2)}, u32[]{:S(2)}) collective-permute-start(f32[4,2,64,256]{3,2,1,0:T(8,128)S(1)} %get-tuple-element.392), channel_id=1, source_target_pairs={{0,2},{2,4},{4,6},{6,8},{8,10},{10,12},{12,14},{1,3},{3,5},{5,7},{... | collective-permute-start | bytes 1572872 | tf_op jit(solution)/shard_map/ppermute | solution.py:32
  13.4 22.7 %collective-permute-start.1 = (f32[4,2,64,256]{3,2,1,0:T(8,128)S(1)}, f32[4,2,64,256]{3,2,1,0:T(8,128)}, u32[]{:S(2)}, u32[]{:S(2)}) collective-permute-start(f32[4,2,64,256]{3,2,1,0:T(8,128)S(1)} %get-tuple-element.393), channel_id=1, source_target_pairs={{2,0},{4,2},{6,4},{8,6},{10,8},{12,10},{14,12},{3,1},{5,3},{7,5},{... | collective-permute-start | bytes 1572872 | tf_op jit(solution)/shard_map/ppermute | solution.py:33
  36.1 6.3 copy-start.25
  37.5 4.9 copy-start.10
  37.5 6.5 copy-start.26
  39.0 11.5 %collective-permute-start.2 = (f32[4,2,256,64]{2,3,1,0:T(8,128)}, f32[4,2,256,64]{2,3,1,0:T(8,128)}, u32[]{:S(2)}, u32[]{:S(2)}) collective-permute-start(f32[4,2,256,64]{2,3,1,0:T(8,128)} %get-tuple-element.388), channel_id=1, source_target_pairs={{0,1},{2,3},{4,5},{6,7},{8,9},{10,11},{12,13},{14,15},{16,17},{18,... | collective-permute-start | bytes 1572872 | tf_op jit(solution)/shard_map/ppermute | solution.py:32
  41.1 9.5 %collective-permute-start.3 = (f32[4,2,256,64]{2,3,1,0:T(8,128)}, f32[4,2,256,64]{2,3,1,0:T(8,128)}, u32[]{:S(2)}, u32[]{:S(2)}) collective-permute-start(f32[4,2,256,64]{2,3,1,0:T(8,128)} %get-tuple-element.389), channel_id=1, source_target_pairs={{1,0},{3,2},{5,4},{7,6},{9,8},{11,10},{13,12},{15,14},{17,16},{19,... | collective-permute-start | bytes 1572872 | tf_op jit(solution)/shard_map/ppermute | solution.py:33
  44.0 6.6 %copy-start.11 = (f32[4,2,64,256]{2,3,1,0:T(8,128)S(1)}, f32[4,2,64,256]{2,3,1,0:T(8,128)}, u32[]{:S(2)}) copy-start(f32[4,2,64,256]{2,3,1,0:T(8,128)} %copy-done.10) | copy-start | bytes 1572868
  56.7 8.8 %copy-start = (f32[8,2,128,128]{2,3,0,1:T(8,128)}, f32[8,2,128,128]{2,3,0,1:T(8,128)S(1)}, u32[]{:S(2)}) copy-start(f32[8,2,128,128]{2,3,0,1:T(8,128)S(1)} %get-tuple-element.634) | copy-start | bytes 3145732 | tf_op jit(solution)/shard_map/while
  63.1 3.4 copy-start.4
  63.1 3.4 copy-start.6
  90.2 4.4 copy-start.2
  90.2 4.4 copy-start.3
  97.0 4.5 copy-start.24
  122.8 3.6 copy-start.5
  122.8 3.6 copy-start.7
  123.4 3.0 copy-start.1
  126.4 2.3 copy-start.13
  126.4 2.3 copy-start.14
  138.7 8.8 %copy-start = (f32[8,2,128,128]{2,3,0,1:T(8,128)}, f32[8,2,128,128]{2,3,0,1:T(8,128)S(1)}, u32[]{:S(2)}) copy-start(f32[8,2,128,128]{2,3,0,1:T(8,128)S(1)} %get-tuple-element.634) | copy-start | bytes 3145732 | tf_op jit(solution)/shard_map/while
  145.2 3.4 copy-start.4
  145.2 3.4 copy-start.6
  172.5 4.4 copy-start.2
  172.5 4.4 copy-start.3
  179.2 4.5 copy-start.24
  205.1 3.6 copy-start.5
  205.1 3.6 copy-start.7
  205.7 3.0 copy-start.1
  208.7 3.7 copy-start.13
  208.7 3.7 copy-start.14
  208.7 3.7 copy-start.15
  208.7 3.7 copy-start.16
  209.8 2.5 copy-start.19
  209.9 2.5 copy-start.20
  209.9 2.5 copy-start.21
  209.9 2.5 copy-start.22
  209.9 2.6 copy-start.17
  209.9 2.6 copy-start.18
  229.2 5.2 copy-start.9
  234.3 110.6 %all-reduce.19.cloned.1.call-start = ((), (), s32[]{:S(2)}) async-start(), calls=%async_computation.1 | async-start | bytes 2097152 | tf_op jit(solution)/shard_map/psum | solution.py:12
  235.6 42.9 %collective-permute-start.4 = (f32[4,2,64,384]{3,2,1,0:T(8,128)}, f32[4,2,64,384]{3,2,1,0:T(8,128)}, u32[]{:S(2)}, u32[]{:S(2)}) collective-permute-start(f32[4,2,64,384]{3,2,1,0:T(8,128)} %get-tuple-element.386), channel_id=1, source_target_pairs={{0,2},{2,4},{4,6},{6,8},{8,10},{10,12},{12,14},{1,3},{3,5},{5,7},{... | collective-permute-start | bytes 2359304 | tf_op jit(solution)/shard_map/ppermute | solution.py:22
  241.5 37.1 %collective-permute-start.5 = (f32[4,2,64,384]{3,2,1,0:T(8,128)}, f32[4,2,64,384]{3,2,1,0:T(8,128)}, u32[]{:S(2)}, u32[]{:S(2)}) collective-permute-start(f32[4,2,64,384]{3,2,1,0:T(8,128)} %get-tuple-element.387), channel_id=1, source_target_pairs={{2,0},{4,2},{6,4},{8,6},{10,8},{12,10},{14,12},{3,1},{5,3},{7,5},{... | collective-permute-start | bytes 2359304 | tf_op jit(solution)/shard_map/ppermute | solution.py:22
  258.6 25.8 %copy-start.23 = (f32[8,2,128,128]{3,2,1,0:T(8,128)S(1)}, f32[8,2,128,128]{3,2,1,0:T(8,128)}, u32[]{:S(2)}) copy-start(f32[8,2,128,128]{3,2,1,0:T(8,128)} %param.8) | copy-start | bytes 3145732
  280.1 3.0 copy-start.12
  280.3 4.8 collective-permute-start.6
  283.1 3.8 collective-permute-start.7
  344.9 8.8 %copy-start.8 = (f32[8,2,16384]{2,0,1:T(8,128)S(1)}, f32[8,2,16384]{2,0,1:T(8,128)}, u32[]{:S(2)}) copy-start(f32[8,2,16384]{2,0,1:T(8,128)} %all-reduce.19.cloned.1.call-done) | copy-start | bytes 3145732
  (8 other events, 11.8 us)
Sparse Core Ops, SparseCore 0:
  234.4 24.1 all-reduce.16
  262.5 82.3 all-reduce.18
